TPU v7x, 32 devices: a whole 2x2x4 slice. The times are simulated.
32 devices in a mesh: group: 4 (over y, x), leaf: 8 (over z, core).
Axes of the slice: x: 2, y: 2, z: 4, core: 2. Of those that a mesh axis runs over, the one named last changes fastest.
Arguments:
- points: bfloat16 [65536, 64], P(('group', 'leaf')), may hold values from -1.1953125 to 1.1953125
- ordering: int32 [32, 2048], P(('group', 'leaf')), may hold values from 0 to 2047, each once within a row
- iterate: float32 [65536, 128], P(('group', 'leaf')), may hold values from -6 to 6
- target: float32 [65536, 128], P(('group', 'leaf')), may hold values from -18 to 18
- step_size: float32 [128], replicated, may hold values from 0.1 to 0.5
- leaf_basis: bfloat16 [65536, 256], P(('group', 'leaf')), may hold values from -0.125 to 0.125
- transfer: bfloat16 [32, 256, 256], P(('group', 'leaf')), may hold values from -0.375 to 0.375
- leaf_skeleton: bfloat16 [32, 256, 64], P(('group', 'leaf')), may hold values from -0.8984375 to 0.8984375
- cluster_skeleton: bfloat16 [4, 256, 64], P('group'), may hold values from -1.1953125 to 1.1953125
- near_table: int32 [32, 8], P(('group', 'leaf')), may hold values from 0 to 1, as said below
- far_table: int32 [32, 8], P(('group', 'leaf')), may hold values from 0 to 1, as said below
- cluster_far: int32 [4, 4], P('group'), may hold values from 0 to 1, as said below
Outputs:
- updated: float32 [65536, 128], P(('group', 'leaf'))
Inputs may be any that keep to these rules, and one draw needn't show every extreme that they name: `near_table`: entries 0 or 1; each leaf's own place is 1; a 1 stands only at places at most 3 away from the leaf's own place; each row has at most 7 ones, and some row exactly 7. `far_table`: entries 0 or 1, never 1 where near_table is 1. `cluster_far`: entries 0 or 1, zero on the diagonal. `ordering`: each row is a permutation.
All inputs are finite; a program needn't handle non-finite values.
Results may differ from a plain program's by a relative error of at most 0.0044.
Values may be sent and summed in bfloat16 or wider, within the bound.
No kernel may reach another device: no remote copies, remote signals or barrier semaphores. Data moves between devices by JAX's collectives and lax.ppermute only.
A program may use at most 128 MiB of HBM per device.

v0:
```python
import jax
import jax.numpy as jnp
from jax import lax
from jax.sharding import PartitionSpec as P

NEAR_MOST = 7


def passed_along(block, axis, distance):
    devices = range(lax.axis_size(axis))
    route = [(i - distance, i) for i in devices if i - distance in devices]
    return lax.ppermute(block, axis, route)


def kernel_tile(left, right):
    left_f = left.astype(jnp.float32)
    right_f = right.astype(jnp.float32)
    left_sq = jnp.sum(left_f * left_f, axis=1)
    right_sq = jnp.sum(right_f * right_f, axis=1)
    inner = lax.dot_general(
        left, right, (((1,), (1,)), ((), ())), preferred_element_type=jnp.float32
    )
    return jnp.exp(-(left_sq[:, None] + right_sq[None, :] - 2.0 * inner)).astype(jnp.bfloat16)


def body(
    points,
    ordering,
    iterate,
    target,
    step_size,
    leaf_basis,
    transfer,
    leaf_skeleton,
    cluster_skeleton,
    near_table,
    far_table,
    cluster_far,
):
    leaf_rows = points.shape[0]
    point_cols = points.shape[1]
    rhs_cols = iterate.shape[1]
    rank_cols = leaf_basis.shape[1]
    rounded = iterate.astype(jnp.bfloat16)
    coeffs = lax.dot_general(
        leaf_basis, rounded, (((0,), (0,)), ((), ())), preferred_element_type=jnp.float32
    ).astype(jnp.bfloat16)
    near_row = near_table[0]
    far_row = far_table[0]
    own_transfer = transfer[0]
    reach = (NEAR_MOST - 1) // 2
    joined = jnp.concatenate([points, rounded], axis=1)
    below_blocks = []
    above_blocks = []
    passing_below = joined
    passing_above = joined
    for distance in range(1, reach + 1):
        passing_below = passed_along(passing_below, "leaf", 1)
        passing_above = passed_along(passing_above, "leaf", -1)
        below_blocks.append(passing_below)
        above_blocks.append(passing_above)
    padded = jnp.concatenate(below_blocks[::-1] + [joined] + above_blocks, axis=0)
    myself = lax.axis_index("leaf")
    cluster_size = near_row.shape[0]

    def window_visit(position, summed):
        place = myself + position - reach
        inside = (place >= 0) & (place < cluster_size)
        listed = lax.dynamic_index_in_dim(
            near_row, jnp.clip(place, 0, cluster_size - 1), 0, keepdims=False
        )
        block = lax.dynamic_slice_in_dim(padded, position * leaf_rows, leaf_rows, 0)
        other_points = block[:, :point_cols]
        other_values = block[:, point_cols:]

        def include(current):
            return current + jnp.dot(
                kernel_tile(points, other_points), other_values, preferred_element_type=jnp.float32
            )

        return lax.cond(inside & (listed > 0), include, lambda current: current, summed)

    near_sum = lax.fori_loop(
        0, 2 * reach + 1, window_visit, jnp.zeros((leaf_rows, rhs_cols), jnp.float32)
    )

    def far_visit(skeletons, values):

        def visit(position, summed):
            listed = lax.dynamic_index_in_dim(far_row, position, 0, keepdims=False)

            def include(current):
                return current + jnp.dot(
                    kernel_tile(leaf_skeleton[0], skeletons[position]),
                    values[position],
                    preferred_element_type=jnp.float32,
                )

            return lax.cond(listed > 0, include, lambda current: current, summed)

        return visit

    empty_far = jnp.zeros((rank_cols, rhs_cols), jnp.float32)
    skeletons = lax.all_gather(leaf_skeleton, "leaf", axis=0, tiled=True)
    values = lax.all_gather(coeffs[None], "leaf", axis=0, tiled=True)
    far_sum = lax.fori_loop(0, skeletons.shape[0], far_visit(skeletons, values), empty_far)
    upward_terms = lax.dot_general(
        own_transfer, coeffs, (((0,), (0,)), ((), ())), preferred_element_type=jnp.float32
    )
    upper = lax.psum(upward_terms, "leaf").astype(jnp.bfloat16)
    cluster_row = cluster_far[0]
    skeletons = lax.all_gather(cluster_skeleton, "group", axis=0, tiled=True)
    values = lax.all_gather(upper[None], "group", axis=0, tiled=True)

    def visit(position, summed):
        listed = lax.dynamic_index_in_dim(cluster_row, position, 0, keepdims=False)

        def include(current):
            return current + jnp.dot(
                kernel_tile(cluster_skeleton[0], skeletons[position]),
                values[position],
                preferred_element_type=jnp.float32,
            )

        return lax.cond(listed > 0, include, lambda current: current, summed)

    lower = lax.fori_loop(0, skeletons.shape[0], visit, empty_far).astype(jnp.bfloat16)
    local = (far_sum + jnp.dot(own_transfer, lower, preferred_element_type=jnp.float32)).astype(
        jnp.bfloat16
    )
    image = jnp.dot(leaf_basis, local, preferred_element_type=jnp.float32) + near_sum
    sorted_target = target[ordering[0]]
    return iterate + step_size[None, :] * (sorted_target - image)


def solution(mesh):
    return jax.shard_map(
        body,
        mesh=mesh,
        in_specs=(
            P(("group", "leaf"), None),
            P(("group", "leaf"), None),
            P(("group", "leaf"), None),
            P(("group", "leaf"), None),
            P(),
            P(("group", "leaf"), None),
            P(("group", "leaf"), None, None),
            P(("group", "leaf"), None, None),
            P("group", None, None),
            P(("group", "leaf"), None),
            P(("group", "leaf"), None),
            P("group", None),
        ),
        out_specs=P(("group", "leaf"), None),
        check_vma=False,
    )
```

profile of v0, /device:TPU:15, one launch (start us, length us, event | category | flops | bytes accessed | tf_op | source)
XLA Modules:
  0.0 278.6 jit_solution(15546868874311557150)
XLA Ops:
  0.0 1.7 copy.46
  2.7 1.9 pad_maximum_fusion
  4.6 3.9 %collective-permute-start = (bf16[2048,192]{0,1:T(8,128)(2,1)}, bf16[2048,192]{0,1:T(8,128)(2,1)}, u32[]{:S(2)}, u32[]{:S(2)}) collective-permute-start(bf16[2048,192]{0,1:T(8,128)(2,1)} %pad_maximum_fusion), channel_id=1, source_target_pairs={{0,1},{1,2},{2,3},{3,4},{4,5},{5,6},{6,7},{8,9},{9,10},{10,11},{11... | collective-permute-start | bytes 2359304 | tf_op jit(solution)/shard_map/ppermute | solution.py:12
  8.5 1.9 collective-permute-start.3
  10.4 7.3 %collective-permute-done = bf16[2048,192]{0,1:T(8,128)(2,1)} collective-permute-done((bf16[2048,192]{0,1:T(8,128)(2,1)}, bf16[2048,192]{0,1:T(8,128)(2,1)}, u32[]{:S(2)}, u32[]{:S(2)}) %collective-permute-start) | collective-permute-done | bytes 786464 | tf_op jit(solution)/shard_map/ppermute | solution.py:12
  17.7 4.4 %collective-permute-start.1 = (bf16[2048,192]{0,1:T(8,128)(2,1)}, bf16[2048,192]{0,1:T(8,128)(2,1)}, u32[]{:S(2)}, u32[]{:S(2)}) collective-permute-start(bf16[2048,192]{0,1:T(8,128)(2,1)} %collective-permute-done), channel_id=1, source_target_pairs={{0,1},{1,2},{2,3},{3,4},{4,5},{5,6},{6,7},{8,9},{9,10},{10,11},{11... | collective-permute-start | bytes 2359304 | tf_op jit(solution)/shard_map/ppermute | solution.py:12
  22.8 25.1 %all-reduce.1 = bf16[256,128]{0,1:T(8,128)(2,1)S(1)} all-reduce(f32[256,128]{0,1:T(8,128)S(1)} %convolution_bitcast_fusion.2), channel_id=1, replica_groups=mesh['group'=4,'leaf'=8] {'leaf'}, use_global_device_ids=true, to_apply=%region_6.7 | all-reduce | flops 32768 | bytes 196608 | tf_op jit(solution)/shard_map/psum | solution.py:110
  47.9 17.8 %all-gather = bf16[2048,128]{1,0:T(8,128)(2,1)} all-gather(bf16[256,128]{1,0:T(8,128)(2,1)S(1)} %convolution_convert_fusion), channel_id=2, replica_groups=mesh['group'=4,'leaf'=8] {'leaf'}, dimensions={0}, use_global_device_ids=true | all-gather | bytes 589824 | tf_op jit(solution)/shard_map/all_gather | solution.py:105
  65.8 2.1 collective-permute-start.4
  67.8 4.1 %collective-permute-start.2 = (bf16[2048,192]{0,1:T(8,128)(2,1)}, bf16[2048,192]{0,1:T(8,128)(2,1)}, u32[]{:S(2)}, u32[]{:S(2)}) collective-permute-start(bf16[2048,192]{0,1:T(8,128)(2,1)} %collective-permute-done.1), channel_id=1, source_target_pairs={{0,1},{1,2},{2,3},{3,4},{4,5},{5,6},{6,7},{8,9},{9,10},{10,11},{11... | collective-permute-start | bytes 2359304 | tf_op jit(solution)/shard_map/ppermute | solution.py:12
  71.9 20.0 %all_gather.12 = bf16[8,256,64]{1,2,0:T(8,128)(2,1)} all-gather(bf16[1,256,64]{1,2,0:T(8,128)(2,1)S(1)} %copy-done.8), channel_id=1, replica_groups=mesh['group'=4,'leaf'=8] {'leaf'}, dimensions={0}, use_global_device_ids=true | all-gather | bytes 294912 | tf_op jit(solution)/shard_map/all_gather | solution.py:104
  93.1 1.9 copy.37
  95.7 17.8 %while.50 = (s32[]{:T(128)}, f32[256,128]{1,0:T(8,128)}, s32[8]{0:T(128)}, bf16[1,256,64]{2,1,0:T(8,128)(2,1)S(1)}, bf16[8,256,64]{2,1,0:T(8,128)(2,1)}, /*index...) while((s32[]{:T(128)}, f32[256,128]{1,0:T(8,128)}, s32[8]{0:T(128)}, bf16[1,256,64]{2,1,0:T(8,128)(2,1)S(1)}, ...), condition=%wide.region_5.6_spmd, body=%wide.region_0.5_spmd.sunk | while | flops 25624072 | bytes 496837 | solution.py:106
  99.4 1.2 dynamic_slice.77
  101.2 1.2 dynamic_slice.77
  103.1 1.2 dynamic_slice.77
  104.9 1.2 dynamic_slice.77
  106.8 1.2 dynamic_slice.77
  110.4 3.1 %conditional.6 = (f32[256,128]{1,0:T(8,128)}) conditional(s32[]{:T(128)} %bitcast.109, f32[256,128]{1,0:T(8,128)} %get-tuple-element.740, (bf16[1,256,64]{2,1,0:T(8,128)(2,1)S(1)}, s32[]{:T(128)}, bf16[8,256,64]{2,1,0:T(8,128)(2,1)}, bf16[8,256,128]{2,1,0:T(8,128)(2,1)}, f32[256,128]{1,0:T(8,128)}) %tuple.135), branch_computations={%region_1.1_spmd, %region_2.4_spmd} | conditional | flops 25624068 | bytes 496686 | solution.py:99
  111.4 2.1 fusion.6
  113.5 1.7 copy.41
  115.2 13.8 %all-gather.1 = bf16[1024,128]{0,1:T(8,128)(2,1)} all-gather(bf16[256,128]{0,1:T(8,128)(2,1)S(1)} %all-reduce.1), channel_id=3, replica_groups=mesh['group'=4,'leaf'=8] {'group'}, dimensions={0}, use_global_device_ids=true | all-gather | bytes 327680 | tf_op jit(solution)/shard_map/all_gather | solution.py:113
  128.9 1.8 copy.48
  131.6 7.2 %all_gather.14 = bf16[4,256,64]{1,2,0:T(8,128)(2,1)} all-gather(bf16[1,256,64]{1,2,0:T(8,128)(2,1)} %param.32), channel_id=1, replica_groups=mesh['group'=4,'leaf'=8] {'group'}, dimensions={0}, use_global_device_ids=true | all-gather | bytes 163840 | tf_op jit(solution)/shard_map/all_gather | solution.py:112
  138.8 1.8 copy.39
  140.6 7.6 %gather_fusion = f32[2048,128]{1,0:T(8,128)} fusion(f32[2048,128]{1,0:T(8,128)S(1)} %copy-done.1, s32[2048]{0:T(1024)S(1)} %broadcast_clamp_fusion), kind=kCustom, calls=%fused_computation | custom fusion | bytes 2105344 | tf_op jit(solution)/shard_map/gather | solution.py:132
  148.2 2.6 copy.45
  150.8 9.8 %while.51 = (s32[]{:T(128)}, f32[256,128]{1,0:T(8,128)S(1)}, s32[4]{0:T(128)S(1)}, bf16[1,256,64]{2,1,0:T(8,128)(2,1)S(1)}, bf16[4,256,64]{2,1,0:T(8,128)(2,1)},...) while((s32[]{:T(128)}, f32[256,128]{1,0:T(8,128)S(1)}, s32[4]{0:T(128)S(1)}, ...), condition=%wide.region_12.13_spmd, body=%wide.region_7.12_spmd.sunk | while | flops 25624072 | bytes 496837 | solution.py:127
  153.4 2.3 conditional.7
  154.4 1.3 fusion.28
  157.0 2.3 conditional.7
  158.0 1.3 fusion.28
  160.7 9.4 %collective-permute-start.5 = (bf16[2048,192]{0,1:T(8,128)(2,1)}, bf16[2048,192]{0,1:T(8,128)(2,1)S(1)}, u32[]{:S(2)}, u32[]{:S(2)}) collective-permute-start(bf16[2048,192]{0,1:T(8,128)(2,1)} %collective-permute-done.4), channel_id=1, source_target_pairs={{1,0},{2,1},{3,2},{4,3},{5,4},{6,5},{7,6},{9,8},{10,9},{11,10},{12... | collective-permute-start | bytes 2359304 | tf_op jit(solution)/shard_map/ppermute | solution.py:12
  170.1 2.2 constant_dynamic-update-slice_fusion.6
  172.3 2.1 constant_dynamic-update-slice_fusion.5
  174.4 2.2 constant_dynamic-update-slice_fusion.4
  177.5 2.2 constant_dynamic-update-slice_fusion.2
  179.7 2.2 constant_dynamic-update-slice_fusion.1
  182.8 9.2 %copy.43 = bf16[14336,192]{1,0:T(8,128)(2,1)} copy(bf16[14336,192]{0,1:T(8,128)(2,1)} %constant_dynamic-update-slice_fusion) | data formatting | bytes 11010048 | tf_op jit(solution)/shard_map/while | solution.py:83
  193.2 77.1 %while.52 = (s32[]{:T(128)}, f32[2048,128]{1,0:T(8,128)}, s32[]{:T(128)}, s32[8]{0:T(128)S(1)}, bf16[2048,64]{1,0:T(8,128)(2,1)S(1)}, /*index=5*/bf16[14336,192]...) while((s32[]{:T(128)}, f32[2048,128]{1,0:T(8,128)}, ...), condition=%wide.region_18.19_spmd, body=%wide.region_13.18_spmd.sunk | while | flops 1632628736 | bytes 3966781 | solution.py:83
  194.5 9.7 %conditional.8 = (f32[2048,128]{1,0:T(8,128)}) conditional(s32[]{:T(128)} %convert_element_type.116, f32[2048,128]{1,0:T(8,128)} %get-tuple-element.708, (bf16[2048,64]{1,0:T(8,128)(2,1)S(1)}, s32[]{:T(128)}, bf16[14336,192]{1,0:T(8,128)(2,1)}, f32[2048,128]{1,0:T(8,128)}) %tuple.139), branch_computations={%region_14.14_spmd, %region_15.17_spmd} | conditional | flops 1632628736 | bytes 3966534 | solution.py:81
  194.5 1.7 multiply_reduce_fusion.4
  196.2 8.0 %convolution_add_fusion = f32[2048,128]{1,0:T(8,128)} fusion(f32[2048,128]{1,0:T(8,128)} %get-tuple-element.471, bf16[2048,64]{1,0:T(8,128)(2,1)S(1)} %get-tuple-element.472, f32[2048]{0:T(1024)S(1)} %get-tuple-element.582, f32[2048]{0:T(1024)S(1)} %get-tuple-element.583, bf16[14336,192]{1,0:T(8,128)(2,1)} %get-tuple-element.473, s32[]{:T(128)S(6)} %select_n.45, ...), kind=kOutput, calls=%fused_computation.47 | convolution fusion | flops 1631846400 | bytes 3425792 | tf_op jit(solution)/shard_map/while/body/eval_jaxpr/cond/branch_1_fun/dot_general | solution.py:77
  205.5 9.7 %conditional.8 = (f32[2048,128]{1,0:T(8,128)}) conditional(s32[]{:T(128)} %convert_element_type.116, f32[2048,128]{1,0:T(8,128)} %get-tuple-element.708, (bf16[2048,64]{1,0:T(8,128)(2,1)S(1)}, s32[]{:T(128)}, bf16[14336,192]{1,0:T(8,128)(2,1)}, f32[2048,128]{1,0:T(8,128)}) %tuple.139), branch_computations={%region_14.14_spmd, %region_15.17_spmd} | conditional | flops 1632628736 | bytes 3966534 | solution.py:81
  205.5 1.7 multiply_reduce_fusion.4
  207.2 8.0 %convolution_add_fusion = f32[2048,128]{1,0:T(8,128)} fusion(f32[2048,128]{1,0:T(8,128)} %get-tuple-element.471, bf16[2048,64]{1,0:T(8,128)(2,1)S(1)} %get-tuple-element.472, f32[2048]{0:T(1024)S(1)} %get-tuple-element.582, f32[2048]{0:T(1024)S(1)} %get-tuple-element.583, bf16[14336,192]{1,0:T(8,128)(2,1)} %get-tuple-element.473, s32[]{:T(128)S(6)} %select_n.45, ...), kind=kOutput, calls=%fused_computation.47 | convolution fusion | flops 1631846400 | bytes 3425792 | tf_op jit(solution)/shard_map/while/body/eval_jaxpr/cond/branch_1_fun/dot_general | solution.py:77
  216.5 9.7 %conditional.8 = (f32[2048,128]{1,0:T(8,128)}) conditional(s32[]{:T(128)} %convert_element_type.116, f32[2048,128]{1,0:T(8,128)} %get-tuple-element.708, (bf16[2048,64]{1,0:T(8,128)(2,1)S(1)}, s32[]{:T(128)}, bf16[14336,192]{1,0:T(8,128)(2,1)}, f32[2048,128]{1,0:T(8,128)}) %tuple.139), branch_computations={%region_14.14_spmd, %region_15.17_spmd} | conditional | flops 1632628736 | bytes 3966534 | solution.py:81
  216.5 1.7 multiply_reduce_fusion.4
  218.2 8.0 %convolution_add_fusion = f32[2048,128]{1,0:T(8,128)} fusion(f32[2048,128]{1,0:T(8,128)} %get-tuple-element.471, bf16[2048,64]{1,0:T(8,128)(2,1)S(1)} %get-tuple-element.472, f32[2048]{0:T(1024)S(1)} %get-tuple-element.582, f32[2048]{0:T(1024)S(1)} %get-tuple-element.583, bf16[14336,192]{1,0:T(8,128)(2,1)} %get-tuple-element.473, s32[]{:T(128)S(6)} %select_n.45, ...), kind=kOutput, calls=%fused_computation.47 | convolution fusion | flops 1631846400 | bytes 3425792 | tf_op jit(solution)/shard_map/while/body/eval_jaxpr/cond/branch_1_fun/dot_general | solution.py:77
  227.5 9.7 %conditional.8 = (f32[2048,128]{1,0:T(8,128)}) conditional(s32[]{:T(128)} %convert_element_type.116, f32[2048,128]{1,0:T(8,128)} %get-tuple-element.708, (bf16[2048,64]{1,0:T(8,128)(2,1)S(1)}, s32[]{:T(128)}, bf16[14336,192]{1,0:T(8,128)(2,1)}, f32[2048,128]{1,0:T(8,128)}) %tuple.139), branch_computations={%region_14.14_spmd, %region_15.17_spmd} | conditional | flops 1632628736 | bytes 3966534 | solution.py:81
  227.5 1.7 multiply_reduce_fusion.4
  229.2 8.0 %convolution_add_fusion = f32[2048,128]{1,0:T(8,128)} fusion(f32[2048,128]{1,0:T(8,128)} %get-tuple-element.471, bf16[2048,64]{1,0:T(8,128)(2,1)S(1)} %get-tuple-element.472, f32[2048]{0:T(1024)S(1)} %get-tuple-element.582, f32[2048]{0:T(1024)S(1)} %get-tuple-element.583, bf16[14336,192]{1,0:T(8,128)(2,1)} %get-tuple-element.473, s32[]{:T(128)S(6)} %select_n.45, ...), kind=kOutput, calls=%fused_computation.47 | convolution fusion | flops 1631846400 | bytes 3425792 | tf_op jit(solution)/shard_map/while/body/eval_jaxpr/cond/branch_1_fun/dot_general | solution.py:77
  238.5 9.7 %conditional.8 = (f32[2048,128]{1,0:T(8,128)}) conditional(s32[]{:T(128)} %convert_element_type.116, f32[2048,128]{1,0:T(8,128)} %get-tuple-element.708, (bf16[2048,64]{1,0:T(8,128)(2,1)S(1)}, s32[]{:T(128)}, bf16[14336,192]{1,0:T(8,128)(2,1)}, f32[2048,128]{1,0:T(8,128)}) %tuple.139), branch_computations={%region_14.14_spmd, %region_15.17_spmd} | conditional | flops 1632628736 | bytes 3966534 | solution.py:81
  238.5 1.7 multiply_reduce_fusion.4
  240.2 8.0 %convolution_add_fusion = f32[2048,128]{1,0:T(8,128)} fusion(f32[2048,128]{1,0:T(8,128)} %get-tuple-element.471, bf16[2048,64]{1,0:T(8,128)(2,1)S(1)} %get-tuple-element.472, f32[2048]{0:T(1024)S(1)} %get-tuple-element.582, f32[2048]{0:T(1024)S(1)} %get-tuple-element.583, bf16[14336,192]{1,0:T(8,128)(2,1)} %get-tuple-element.473, s32[]{:T(128)S(6)} %select_n.45, ...), kind=kOutput, calls=%fused_computation.47 | convolution fusion | flops 1631846400 | bytes 3425792 | tf_op jit(solution)/shard_map/while/body/eval_jaxpr/cond/branch_1_fun/dot_general | solution.py:77
  249.5 9.7 %conditional.8 = (f32[2048,128]{1,0:T(8,128)}) conditional(s32[]{:T(128)} %convert_element_type.116, f32[2048,128]{1,0:T(8,128)} %get-tuple-element.708, (bf16[2048,64]{1,0:T(8,128)(2,1)S(1)}, s32[]{:T(128)}, bf16[14336,192]{1,0:T(8,128)(2,1)}, f32[2048,128]{1,0:T(8,128)}) %tuple.139), branch_computations={%region_14.14_spmd, %region_15.17_spmd} | conditional | flops 1632628736 | bytes 3966534 | solution.py:81
  249.5 1.7 multiply_reduce_fusion.4
  251.2 8.1 %convolution_add_fusion = f32[2048,128]{1,0:T(8,128)} fusion(f32[2048,128]{1,0:T(8,128)} %get-tuple-element.471, bf16[2048,64]{1,0:T(8,128)(2,1)S(1)} %get-tuple-element.472, f32[2048]{0:T(1024)S(1)} %get-tuple-element.582, f32[2048]{0:T(1024)S(1)} %get-tuple-element.583, bf16[14336,192]{1,0:T(8,128)(2,1)} %get-tuple-element.473, s32[]{:T(128)S(6)} %select_n.45, ...), kind=kOutput, calls=%fused_computation.47 | convolution fusion | flops 1631846400 | bytes 3425792 | tf_op jit(solution)/shard_map/while/body/eval_jaxpr/cond/branch_1_fun/dot_general | solution.py:77
  260.5 9.8 %conditional.8 = (f32[2048,128]{1,0:T(8,128)}) conditional(s32[]{:T(128)} %convert_element_type.116, f32[2048,128]{1,0:T(8,128)} %get-tuple-element.708, (bf16[2048,64]{1,0:T(8,128)(2,1)S(1)}, s32[]{:T(128)}, bf16[14336,192]{1,0:T(8,128)(2,1)}, f32[2048,128]{1,0:T(8,128)}) %tuple.139), branch_computations={%region_14.14_spmd, %region_15.17_spmd} | conditional | flops 1632628736 | bytes 3966534 | solution.py:81
  260.5 1.7 multiply_reduce_fusion.4
  262.2 8.1 %convolution_add_fusion = f32[2048,128]{1,0:T(8,128)} fusion(f32[2048,128]{1,0:T(8,128)} %get-tuple-element.471, bf16[2048,64]{1,0:T(8,128)(2,1)S(1)} %get-tuple-element.472, f32[2048]{0:T(1024)S(1)} %get-tuple-element.582, f32[2048]{0:T(1024)S(1)} %get-tuple-element.583, bf16[14336,192]{1,0:T(8,128)(2,1)} %get-tuple-element.473, s32[]{:T(128)S(6)} %select_n.45, ...), kind=kOutput, calls=%fused_computation.47 | convolution fusion | flops 1631846400 | bytes 3425792 | tf_op jit(solution)/shard_map/while/body/eval_jaxpr/cond/branch_1_fun/dot_general | solution.py:77
  270.3 2.5 copy.44
  272.9 3.2 %fusion.56 = f32[2048,128]{0,1:T(8,128)} fusion(f32[2048,128]{0,1:T(8,128)S(1)} %copy-done.3, f32[2048,128]{0,1:T(8,128)} %copy.45, f32[2048,128]{0,1:T(8,128)} %copy.44, bf16[2048,256]{1,0:T(8,128)(2,1)S(1)} %copy-done, f32[256,128]{0,1:T(8,128)S(1)} %copy-done.7, f32[128]{0:T(128)S(1)} %copy-done.10, bf16[1,256,256]{2,1,0:T(8,128)(2,1)S(1)} %copy-done.6, ...), kind=kOutput, calls=%fused_computation.58 | convolution fusion | flops 152141824 | bytes 5636608 | tf_op jit(solution)/shard_map/dot_general | solution.py:131
  276.1 2.5 copy.47
  (70 shorter events, 21.1 us)
Async XLA Ops:
  0.0 22.1 %copy-start = (bf16[2048,256]{1,0:T(8,128)(2,1)S(1)}, bf16[2048,256]{1,0:T(8,128)(2,1)}, u32[]{:S(2)}) copy-start(bf16[2048,256]{1,0:T(8,128)(2,1)} %param.29) | copy-start | bytes 3145732
  0.0 91.9 %copy-start.4 = (bf16[2048,64]{0,1:T(8,128)(2,1)S(1)}, bf16[2048,64]{0,1:T(8,128)(2,1)}, u32[]{:S(2)}) copy-start(bf16[2048,64]{0,1:T(8,128)(2,1)} %param.24) | copy-start | bytes 786436
  0.0 22.6 %copy-start.5 = (bf16[1,256,256]{2,1,0:T(8,128)(2,1)S(1)}, bf16[1,256,256]{2,1,0:T(8,128)(2,1)}, u32[]{:S(2)}) copy-start(bf16[1,256,256]{2,1,0:T(8,128)(2,1)} %param.30) | copy-start | bytes 393220
  0.0 71.9 %copy-start.8 = (bf16[1,256,64]{1,2,0:T(8,128)(2,1)S(1)}, bf16[1,256,64]{1,2,0:T(8,128)(2,1)}, u32[]{:S(2)}) copy-start(bf16[1,256,64]{1,2,0:T(8,128)(2,1)} %param.31) | copy-start | bytes 98308
  1.7 1.0 copy-start.2
  2.7 137.9 %copy-start.9 = (s32[1,2048]{1,0:T(1,128)S(1)}, s32[1,2048]{1,0:T(1,128)}, u32[]{:S(2)}) copy-start(s32[1,2048]{1,0:T(1,128)} %param.25) | copy-start | bytes 24580
  4.6 136.0 %copy-start.1 = (f32[2048,128]{1,0:T(8,128)S(1)}, f32[2048,128]{1,0:T(8,128)}, u32[]{:S(2)}) copy-start(f32[2048,128]{1,0:T(8,128)} %param.27) | copy-start | bytes 3145732
  4.6 13.1 %collective-permute-start = (bf16[2048,192]{0,1:T(8,128)(2,1)}, bf16[2048,192]{0,1:T(8,128)(2,1)}, u32[]{:S(2)}, u32[]{:S(2)}) collective-permute-start(bf16[2048,192]{0,1:T(8,128)(2,1)} %pad_maximum_fusion), channel_id=1, source_target_pairs={{0,1},{1,2},{2,3},{3,4},{4,5},{5,6},{6,7},{8,9},{9,10},{10,11},{11... | collective-permute-start | bytes 2359304 | tf_op jit(solution)/shard_map/ppermute | solution.py:12
  8.5 57.3 %collective-permute-start.3 = (bf16[2048,192]{0,1:T(8,128)(2,1)}, bf16[2048,192]{0,1:T(8,128)(2,1)}, u32[]{:S(2)}, u32[]{:S(2)}) collective-permute-start(bf16[2048,192]{0,1:T(8,128)(2,1)} %pad_maximum_fusion), channel_id=1, source_target_pairs={{1,0},{2,1},{3,2},{4,3},{5,4},{6,5},{7,6},{9,8},{10,9},{11,10},{12... | collective-permute-start | bytes 2359304 | tf_op jit(solution)/shard_map/ppermute | solution.py:12
  17.7 50.1 %collective-permute-start.1 = (bf16[2048,192]{0,1:T(8,128)(2,1)}, bf16[2048,192]{0,1:T(8,128)(2,1)}, u32[]{:S(2)}, u32[]{:S(2)}) collective-permute-start(bf16[2048,192]{0,1:T(8,128)(2,1)} %collective-permute-done), channel_id=1, source_target_pairs={{0,1},{1,2},{2,3},{3,4},{4,5},{5,6},{6,7},{8,9},{9,10},{10,11},{11... | collective-permute-start | bytes 2359304 | tf_op jit(solution)/shard_map/ppermute | solution.py:12
  65.8 94.9 %collective-permute-start.4 = (bf16[2048,192]{0,1:T(8,128)(2,1)}, bf16[2048,192]{0,1:T(8,128)(2,1)}, u32[]{:S(2)}, u32[]{:S(2)}) collective-permute-start(bf16[2048,192]{0,1:T(8,128)(2,1)} %collective-permute-done.3), channel_id=1, source_target_pairs={{1,0},{2,1},{3,2},{4,3},{5,4},{6,5},{7,6},{9,8},{10,9},{11,10},{12... | collective-permute-start | bytes 2359304 | tf_op jit(solution)/shard_map/ppermute | solution.py:12
  67.8 102.2 %collective-permute-start.2 = (bf16[2048,192]{0,1:T(8,128)(2,1)}, bf16[2048,192]{0,1:T(8,128)(2,1)}, u32[]{:S(2)}, u32[]{:S(2)}) collective-permute-start(bf16[2048,192]{0,1:T(8,128)(2,1)} %collective-permute-done.1), channel_id=1, source_target_pairs={{0,1},{1,2},{2,3},{3,4},{4,5},{5,6},{6,7},{8,9},{9,10},{10,11},{11... | collective-permute-start | bytes 2359304 | tf_op jit(solution)/shard_map/ppermute | solution.py:12
  140.6 10.2 %copy-start.11 = (s32[1,4]{1,0:T(1,128)S(1)}, s32[1,4]{1,0:T(1,128)}, u32[]{:S(2)}) copy-start(s32[1,4]{1,0:T(1,128)} %param.35) | copy-start | bytes 52
  160.7 21.2 %collective-permute-start.5 = (bf16[2048,192]{0,1:T(8,128)(2,1)}, bf16[2048,192]{0,1:T(8,128)(2,1)S(1)}, u32[]{:S(2)}, u32[]{:S(2)}) collective-permute-start(bf16[2048,192]{0,1:T(8,128)(2,1)} %collective-permute-done.4), channel_id=1, source_target_pairs={{1,0},{2,1},{3,2},{4,3},{5,4},{6,5},{7,6},{9,8},{10,9},{11,10},{12... | collective-permute-start | bytes 2359304 | tf_op jit(solution)/shard_map/ppermute | solution.py:12
  182.8 10.3 %copy-start.12 = (s32[1,8]{1,0:T(1,128)S(1)}, s32[1,8]{1,0:T(1,128)}, u32[]{:S(2)}) copy-start(s32[1,8]{1,0:T(1,128)} %param.33) | copy-start | bytes 100
  193.1 79.7 %copy-start.3 = (f32[2048,128]{0,1:T(8,128)S(1)}, f32[2048,128]{0,1:T(8,128)}, u32[]{:S(2)}) copy-start(f32[2048,128]{0,1:T(8,128)} %copy-done.2) | copy-start | bytes 3145732
  193.1 79.7 %copy-start.6 = (bf16[1,256,256]{2,1,0:T(8,128)(2,1)S(1)}, bf16[1,256,256]{2,1,0:T(8,128)(2,1)}, u32[]{:S(2)}) copy-start(bf16[1,256,256]{2,1,0:T(8,128)(2,1)} %param.30) | copy-start | bytes 393220
  193.1 79.7 %copy-start.7 = (f32[256,128]{0,1:T(8,128)S(1)}, f32[256,128]{0,1:T(8,128)}, u32[]{:S(2)}) copy-start(f32[256,128]{0,1:T(8,128)} %copy.41) | copy-start | bytes 393220
  193.2 79.7 %copy-start.10 = (f32[128]{0:T(128)S(1)}, f32[128]{0:T(128)}, u32[]{:S(2)}) copy-start(f32[128]{0:T(128)} %param.28) | copy-start | bytes 1540
where the time goes:
time: 281 us; the launch traced here: 279 us
  blocking collectives  84 us (30%)
  local copies, waits for them, and re-layouts  66.5 us (24%)
  matrix products  65 us (23%)
  starting transfers between devices  25.7 us (9%)
  other arithmetic  17.5 us (6%)
  loops' own time  12.3 us (4%)
  waiting for transfers between devices  7.31 us (3%)
    dot_general x7, matrix products, include(): jnp.dot(kernel_tile(points, other_points), other_values, preferred_elemen...  56.4 us
    ppermute x6, starting transfers between devices, passed_along(): return lax.ppermute(block, axis, route)  25.7 us
    psum x1, blocking collectives, body(): upper = lax.psum(upward_terms, 'leaf').astype(jnp.bfloat16)  25.1 us
    all_gather x1, blocking collectives, body(): skeletons = lax.all_gather(leaf_skeleton, 'leaf', axis=0, tiled=True)  20 us
    all_gather x1, blocking collectives, body(): values = lax.all_gather(coeffs[None], 'leaf', axis=0, tiled=True)  17.8 us
    reduce_sum x10, other arithmetic, kernel_tile(): right_sq = jnp.sum(right_f * right_f, axis=1)  14.6 us
    all_gather x1, blocking collectives, body(): values = lax.all_gather(upper[None], 'group', axis=0, tiled=True)  13.8 us
    unnamed x32, local copies, waits for them, and re-layouts  13.4 us
  transfers between devices with their start and end apart: 6, of which 1 were waited for; matrix products, arithmetic and copies ran while one was open for 19% of the time, Pallas kernels for 0%

commit v1 on v0

--- a/solution.py
+++ b/solution.py
@@ -107,7 +107,7 @@
     upward_terms = lax.dot_general(
         own_transfer, coeffs, (((0,), (0,)), ((), ())), preferred_element_type=jnp.float32
     )
-    upper = lax.psum(upward_terms, "leaf").astype(jnp.bfloat16)
+    upper = jnp.sum(lax.all_gather(upward_terms, "leaf"), axis=0).astype(jnp.bfloat16)
     cluster_row = cluster_far[0]
     skeletons = lax.all_gather(cluster_skeleton, "group", axis=0, tiled=True)
     values = lax.all_gather(upper[None], "group", axis=0, tiled=True)

time: 281 us -> 259 us (0.922)
  blocking collectives: 84 us -> 51.4 us
  between operations: 0.26 us -> 13.7 us
    psum x1 -> x0, blocking collectives: 25.1 us -> none  [body(): upper = lax.psum(upward_terms, 'leaf').astype(jnp.bfloat16)]
    all_gather x1, blocking collectives: 13.8 us -> 8.05 us  [body(): values = lax.all_gather(upper[None], 'group', axis=0, tiled=True)]
    unnamed x32 -> x37, local copies, waits for them, and re-layouts: 13.4 us -> 14.8 us
  transfers between devices with their start and end apart: 6 -> 7, of which waited for: 1 -> 1; matrix products, arithmetic and copies ran while one was open for 19% -> 19% of each run, Pallas kernels for 0% -> 0%
where the time goes in v1:
time: 259 us; the launch traced here: 257 us
  local copies, waits for them, and re-layouts  67.1 us (26%)
  matrix products  63.9 us (25%)
  blocking collectives  51.4 us (20%)
  starting transfers between devices  25.3 us (10%)
  other arithmetic  16.2 us (6%)
  between operations  13.7 us (5%)
  loops' own time  13.2 us (5%)
  waiting for transfers between devices  5.96 us (2%)
    dot_general x7, matrix products, include(): jnp.dot(kernel_tile(points, other_points), other_values, preferred_elemen...  56.3 us
    ppermute x6, starting transfers between devices, passed_along(): return lax.ppermute(block, axis, route)  25.3 us
    all_gather x1, blocking collectives, body(): skeletons = lax.all_gather(leaf_skeleton, 'leaf', axis=0, tiled=True)  20.3 us
    all_gather x1, blocking collectives, body(): values = lax.all_gather(coeffs[None], 'leaf', axis=0, tiled=True)  16.1 us
    unnamed x37, local copies, waits for them, and re-layouts  14.8 us
    reduce_sum x10, other arithmetic, kernel_tile(): right_sq = jnp.sum(right_f * right_f, axis=1)  12.9 us
    while x3, local copies, waits for them, and re-layouts, body(): lax.fori_loop(0, 2 * reach + 1, window_visit, jnp.zeros((leaf_rows, rhs_c...  12.1 us
    dynamic_slice x8, local copies, waits for them, and re-layouts, visit(): listed = lax.dynamic_index_in_dim(far_row, position, 0, keepdims=False)  10.6 us
  transfers between devices with their start and end apart: 7, of which 1 were waited for; matrix products, arithmetic and copies ran while one was open for 19% of the time, Pallas kernels for 0%

profile of v1, /device:TPU:15, one launch (start us, length us, event | category | flops | bytes accessed | tf_op | source)
XLA Modules:
  0.0 256.7 jit_solution(9671115431353544800)
XLA Ops:
  6.6 1.7 copy.44
  9.3 2.0 pad_maximum_fusion
  11.3 3.8 %collective-permute-start = (bf16[2048,192]{0,1:T(8,128)(2,1)}, bf16[2048,192]{0,1:T(8,128)(2,1)}, u32[]{:S(2)}, u32[]{:S(2)}) collective-permute-start(bf16[2048,192]{0,1:T(8,128)(2,1)} %pad_maximum_fusion), channel_id=1, source_target_pairs={{0,1},{1,2},{2,3},{3,4},{4,5},{5,6},{6,7},{8,9},{9,10},{10,11},{11... | collective-permute-start | bytes 2359304 | tf_op jit(solution)/shard_map/ppermute | solution.py:12
  16.5 1.9 collective-permute-start.3
  18.4 5.9 %collective-permute-done = bf16[2048,192]{0,1:T(8,128)(2,1)} collective-permute-done((bf16[2048,192]{0,1:T(8,128)(2,1)}, bf16[2048,192]{0,1:T(8,128)(2,1)}, u32[]{:S(2)}, u32[]{:S(2)}) %collective-permute-start) | collective-permute-done | bytes 786464 | tf_op jit(solution)/shard_map/ppermute | solution.py:12
  24.3 4.4 %collective-permute-start.1 = (bf16[2048,192]{0,1:T(8,128)(2,1)}, bf16[2048,192]{0,1:T(8,128)(2,1)}, u32[]{:S(2)}, u32[]{:S(2)}) collective-permute-start(bf16[2048,192]{0,1:T(8,128)(2,1)} %collective-permute-done), channel_id=1, source_target_pairs={{0,1},{1,2},{2,3},{3,4},{4,5},{5,6},{6,7},{8,9},{9,10},{10,11},{11... | collective-permute-start | bytes 2359304 | tf_op jit(solution)/shard_map/ppermute | solution.py:12
  29.1 7.0 %all_gather.20 = bf16[4,256,64]{1,2,0:T(8,128)(2,1)} all-gather(bf16[1,256,64]{1,2,0:T(8,128)(2,1)S(1)} %copy-done.10), channel_id=1, replica_groups=mesh['group'=4,'leaf'=8] {'group'}, dimensions={0}, use_global_device_ids=true | all-gather | bytes 163840 | tf_op jit(solution)/shard_map/all_gather | solution.py:112
  36.1 1.8 copy.37
  38.7 16.1 %all-gather = bf16[2048,128]{1,0:T(8,128)(2,1)} all-gather(bf16[256,128]{1,0:T(8,128)(2,1)} %copy-done.6), channel_id=2, replica_groups=mesh['group'=4,'leaf'=8] {'leaf'}, dimensions={0}, use_global_device_ids=true | all-gather | bytes 589824 | tf_op jit(solution)/shard_map/all_gather | solution.py:105
  54.8 2.1 collective-permute-start.4
  56.9 20.3 %all_gather.18 = bf16[8,256,64]{1,2,0:T(8,128)(2,1)} all-gather(bf16[1,256,64]{1,2,0:T(8,128)(2,1)} %param.31), channel_id=1, replica_groups=mesh['group'=4,'leaf'=8] {'leaf'}, dimensions={0}, use_global_device_ids=true | all-gather | bytes 294912 | tf_op jit(solution)/shard_map/all_gather | solution.py:104
  77.2 2.0 copy.35
  79.8 19.5 %while.50 = (s32[]{:T(128)}, f32[256,128]{1,0:T(8,128)}, s32[8]{0:T(128)}, bf16[1,256,64]{2,1,0:T(8,128)(2,1)S(1)}, bf16[8,256,64]{2,1,0:T(8,128)(2,1)}, /*index...) while((s32[]{:T(128)}, f32[256,128]{1,0:T(8,128)}, s32[8]{0:T(128)}, bf16[1,256,64]{2,1,0:T(8,128)(2,1)S(1)}, ...), condition=%wide.region_5.6_spmd, body=%wide.region_0.5_spmd.sunk | while | flops 25624072 | bytes 496837 | solution.py:106
  79.8 1.3 dynamic_slice.77
  81.9 1.3 dynamic_slice.77
  83.9 1.3 dynamic_slice.77
  85.9 1.3 dynamic_slice.77
  88.0 1.3 dynamic_slice.77
  90.0 1.3 dynamic_slice.77
  92.1 1.3 dynamic_slice.77
  94.1 1.3 dynamic_slice.77
  96.2 3.1 %conditional.6 = (f32[256,128]{1,0:T(8,128)}) conditional(s32[]{:T(128)} %bitcast.114, f32[256,128]{1,0:T(8,128)} %get-tuple-element.740, (bf16[1,256,64]{2,1,0:T(8,128)(2,1)S(1)}, s32[]{:T(128)}, bf16[8,256,64]{2,1,0:T(8,128)(2,1)}, bf16[8,256,128]{2,1,0:T(8,128)(2,1)}, f32[256,128]{1,0:T(8,128)}) %tuple.135), branch_computations={%region_1.1_spmd, %region_2.4_spmd} | conditional | flops 25624068 | bytes 496686 | solution.py:99
  97.2 2.1 fusion.6
  99.3 1.6 copy.39
  100.9 7.8 %collective-permute-start.2 = (bf16[2048,192]{0,1:T(8,128)(2,1)}, bf16[2048,192]{0,1:T(8,128)(2,1)}, u32[]{:S(2)}, u32[]{:S(2)}) collective-permute-start(bf16[2048,192]{0,1:T(8,128)(2,1)} %collective-permute-done.1), channel_id=1, source_target_pairs={{0,1},{1,2},{2,3},{3,4},{4,5},{5,6},{6,7},{8,9},{9,10},{10,11},{11... | collective-permute-start | bytes 2359304 | tf_op jit(solution)/shard_map/ppermute | solution.py:12
  108.8 7.6 %gather_fusion = f32[2048,128]{1,0:T(8,128)} fusion(f32[2048,128]{1,0:T(8,128)S(1)} %copy-done.1, s32[2048]{0:T(1024)S(1)} %broadcast_clamp_fusion), kind=kCustom, calls=%fused_computation | custom fusion | bytes 2105344 | tf_op jit(solution)/shard_map/gather | solution.py:132
  116.4 2.6 %copy.43 = f32[2048,128]{0,1:T(8,128)} copy(f32[2048,128]{1,0:T(8,128)} %gather_fusion) | data formatting | bytes 2097152 | tf_op jit(solution)/shard_map/gather | solution.py:132
  119.0 5.4 %collective-permute-start.5 = (bf16[2048,192]{0,1:T(8,128)(2,1)}, bf16[2048,192]{0,1:T(8,128)(2,1)}, u32[]{:S(2)}, u32[]{:S(2)}) collective-permute-start(bf16[2048,192]{0,1:T(8,128)(2,1)} %collective-permute-done.4), channel_id=1, source_target_pairs={{1,0},{2,1},{3,2},{4,3},{5,4},{6,5},{7,6},{9,8},{10,9},{11,10},{12... | collective-permute-start | bytes 2359304 | tf_op jit(solution)/shard_map/ppermute | solution.py:12
  124.4 1.6 copy.47
  126.2 8.0 %all-gather.2 = bf16[1024,128]{0,1:T(8,128)(2,1)S(1)} all-gather(bf16[256,128]{0,1:T(8,128)(2,1)S(1)} %bitcast_reduce_fusion), channel_id=4, replica_groups=mesh['group'=4,'leaf'=8] {'group'}, dimensions={0}, use_global_device_ids=true | all-gather | bytes 327680 | tf_op jit(solution)/shard_map/all_gather | solution.py:113
  134.5 6.3 %while.51 = (s32[]{:T(128)}, f32[256,128]{1,0:T(8,128)S(1)}, s32[4]{0:T(128)S(1)}, bf16[1,256,64]{2,1,0:T(8,128)(2,1)S(1)}, bf16[4,256,64]{2,1,0:T(8,128)(2,1)S(...) while((s32[]{:T(128)}, f32[256,128]{1,0:T(8,128)S(1)}, s32[4]{0:T(128)S(1)}, ...), condition=%wide.region_12.13_spmd, body=%wide.region_7.12_spmd.sunk | while | flops 25624072 | bytes 529605 | solution.py:127
  140.8 2.1 constant_dynamic-update-slice_fusion.6
  142.9 2.1 constant_dynamic-update-slice_fusion.5
  145.0 2.1 constant_dynamic-update-slice_fusion.4
  148.0 2.1 constant_dynamic-update-slice_fusion.2
  150.1 2.1 constant_dynamic-update-slice_fusion.1
  152.3 2.1 constant_dynamic-update-slice_fusion
  154.4 9.3 %copy.41 = bf16[14336,192]{1,0:T(8,128)(2,1)} copy(bf16[14336,192]{0,1:T(8,128)(2,1)} %constant_dynamic-update-slice_fusion) | data formatting | bytes 11010048 | tf_op jit(solution)/shard_map/while | solution.py:83
  163.7 1.1 broadcast_in_dim.12
  164.8 76.8 %while.52 = (s32[]{:T(128)}, f32[2048,128]{1,0:T(8,128)}, s32[]{:T(128)}, s32[8]{0:T(128)S(1)}, bf16[2048,64]{1,0:T(8,128)(2,1)S(1)}, /*index=5*/bf16[14336,192]...) while((s32[]{:T(128)}, f32[2048,128]{1,0:T(8,128)}, ...), condition=%wide.region_18.19_spmd, body=%wide.region_13.18_spmd.sunk | while | flops 1632628736 | bytes 3966781 | solution.py:83
  166.0 9.7 %conditional.8 = (f32[2048,128]{1,0:T(8,128)}) conditional(s32[]{:T(128)} %convert_element_type.127, f32[2048,128]{1,0:T(8,128)} %get-tuple-element.708, (bf16[2048,64]{1,0:T(8,128)(2,1)S(1)}, s32[]{:T(128)}, bf16[14336,192]{1,0:T(8,128)(2,1)}, f32[2048,128]{1,0:T(8,128)}) %tuple.139), branch_computations={%region_14.14_spmd, %region_15.17_spmd} | conditional | flops 1632628736 | bytes 3966534 | solution.py:81
  166.0 1.7 multiply_reduce_fusion.4
  167.7 8.0 %convolution_add_fusion = f32[2048,128]{1,0:T(8,128)} fusion(f32[2048,128]{1,0:T(8,128)} %get-tuple-element.471, bf16[2048,64]{1,0:T(8,128)(2,1)S(1)} %get-tuple-element.472, f32[2048]{0:T(1024)S(1)} %get-tuple-element.582, f32[2048]{0:T(1024)S(1)} %get-tuple-element.583, bf16[14336,192]{1,0:T(8,128)(2,1)} %get-tuple-element.473, s32[]{:T(128)S(6)} %select_n.45, ...), kind=kOutput, calls=%fused_computation.47 | convolution fusion | flops 1631846400 | bytes 3425792 | tf_op jit(solution)/shard_map/while/body/eval_jaxpr/cond/branch_1_fun/dot_general | solution.py:77
  177.0 9.7 %conditional.8 = (f32[2048,128]{1,0:T(8,128)}) conditional(s32[]{:T(128)} %convert_element_type.127, f32[2048,128]{1,0:T(8,128)} %get-tuple-element.708, (bf16[2048,64]{1,0:T(8,128)(2,1)S(1)}, s32[]{:T(128)}, bf16[14336,192]{1,0:T(8,128)(2,1)}, f32[2048,128]{1,0:T(8,128)}) %tuple.139), branch_computations={%region_14.14_spmd, %region_15.17_spmd} | conditional | flops 1632628736 | bytes 3966534 | solution.py:81
  177.0 1.7 multiply_reduce_fusion.4
  178.7 8.0 %convolution_add_fusion = f32[2048,128]{1,0:T(8,128)} fusion(f32[2048,128]{1,0:T(8,128)} %get-tuple-element.471, bf16[2048,64]{1,0:T(8,128)(2,1)S(1)} %get-tuple-element.472, f32[2048]{0:T(1024)S(1)} %get-tuple-element.582, f32[2048]{0:T(1024)S(1)} %get-tuple-element.583, bf16[14336,192]{1,0:T(8,128)(2,1)} %get-tuple-element.473, s32[]{:T(128)S(6)} %select_n.45, ...), kind=kOutput, calls=%fused_computation.47 | convolution fusion | flops 1631846400 | bytes 3425792 | tf_op jit(solution)/shard_map/while/body/eval_jaxpr/cond/branch_1_fun/dot_general | solution.py:77
  188.0 9.7 %conditional.8 = (f32[2048,128]{1,0:T(8,128)}) conditional(s32[]{:T(128)} %convert_element_type.127, f32[2048,128]{1,0:T(8,128)} %get-tuple-element.708, (bf16[2048,64]{1,0:T(8,128)(2,1)S(1)}, s32[]{:T(128)}, bf16[14336,192]{1,0:T(8,128)(2,1)}, f32[2048,128]{1,0:T(8,128)}) %tuple.139), branch_computations={%region_14.14_spmd, %region_15.17_spmd} | conditional | flops 1632628736 | bytes 3966534 | solution.py:81
  188.0 1.7 multiply_reduce_fusion.4
  189.6 8.0 %convolution_add_fusion = f32[2048,128]{1,0:T(8,128)} fusion(f32[2048,128]{1,0:T(8,128)} %get-tuple-element.471, bf16[2048,64]{1,0:T(8,128)(2,1)S(1)} %get-tuple-element.472, f32[2048]{0:T(1024)S(1)} %get-tuple-element.582, f32[2048]{0:T(1024)S(1)} %get-tuple-element.583, bf16[14336,192]{1,0:T(8,128)(2,1)} %get-tuple-element.473, s32[]{:T(128)S(6)} %select_n.45, ...), kind=kOutput, calls=%fused_computation.47 | convolution fusion | flops 1631846400 | bytes 3425792 | tf_op jit(solution)/shard_map/while/body/eval_jaxpr/cond/branch_1_fun/dot_general | solution.py:77
  198.9 9.7 %conditional.8 = (f32[2048,128]{1,0:T(8,128)}) conditional(s32[]{:T(128)} %convert_element_type.127, f32[2048,128]{1,0:T(8,128)} %get-tuple-element.708, (bf16[2048,64]{1,0:T(8,128)(2,1)S(1)}, s32[]{:T(128)}, bf16[14336,192]{1,0:T(8,128)(2,1)}, f32[2048,128]{1,0:T(8,128)}) %tuple.139), branch_computations={%region_14.14_spmd, %region_15.17_spmd} | conditional | flops 1632628736 | bytes 3966534 | solution.py:81
  198.9 1.7 multiply_reduce_fusion.4
  200.6 8.0 %convolution_add_fusion = f32[2048,128]{1,0:T(8,128)} fusion(f32[2048,128]{1,0:T(8,128)} %get-tuple-element.471, bf16[2048,64]{1,0:T(8,128)(2,1)S(1)} %get-tuple-element.472, f32[2048]{0:T(1024)S(1)} %get-tuple-element.582, f32[2048]{0:T(1024)S(1)} %get-tuple-element.583, bf16[14336,192]{1,0:T(8,128)(2,1)} %get-tuple-element.473, s32[]{:T(128)S(6)} %select_n.45, ...), kind=kOutput, calls=%fused_computation.47 | convolution fusion | flops 1631846400 | bytes 3425792 | tf_op jit(solution)/shard_map/while/body/eval_jaxpr/cond/branch_1_fun/dot_general | solution.py:77
  209.9 9.7 %conditional.8 = (f32[2048,128]{1,0:T(8,128)}) conditional(s32[]{:T(128)} %convert_element_type.127, f32[2048,128]{1,0:T(8,128)} %get-tuple-element.708, (bf16[2048,64]{1,0:T(8,128)(2,1)S(1)}, s32[]{:T(128)}, bf16[14336,192]{1,0:T(8,128)(2,1)}, f32[2048,128]{1,0:T(8,128)}) %tuple.139), branch_computations={%region_14.14_spmd, %region_15.17_spmd} | conditional | flops 1632628736 | bytes 3966534 | solution.py:81
  209.9 1.7 multiply_reduce_fusion.4
  211.6 8.0 %convolution_add_fusion = f32[2048,128]{1,0:T(8,128)} fusion(f32[2048,128]{1,0:T(8,128)} %get-tuple-element.471, bf16[2048,64]{1,0:T(8,128)(2,1)S(1)} %get-tuple-element.472, f32[2048]{0:T(1024)S(1)} %get-tuple-element.582, f32[2048]{0:T(1024)S(1)} %get-tuple-element.583, bf16[14336,192]{1,0:T(8,128)(2,1)} %get-tuple-element.473, s32[]{:T(128)S(6)} %select_n.45, ...), kind=kOutput, calls=%fused_computation.47 | convolution fusion | flops 1631846400 | bytes 3425792 | tf_op jit(solution)/shard_map/while/body/eval_jaxpr/cond/branch_1_fun/dot_general | solution.py:77
  220.8 9.7 %conditional.8 = (f32[2048,128]{1,0:T(8,128)}) conditional(s32[]{:T(128)} %convert_element_type.127, f32[2048,128]{1,0:T(8,128)} %get-tuple-element.708, (bf16[2048,64]{1,0:T(8,128)(2,1)S(1)}, s32[]{:T(128)}, bf16[14336,192]{1,0:T(8,128)(2,1)}, f32[2048,128]{1,0:T(8,128)}) %tuple.139), branch_computations={%region_14.14_spmd, %region_15.17_spmd} | conditional | flops 1632628736 | bytes 3966534 | solution.py:81
  220.9 1.7 multiply_reduce_fusion.4
  222.5 8.0 %convolution_add_fusion = f32[2048,128]{1,0:T(8,128)} fusion(f32[2048,128]{1,0:T(8,128)} %get-tuple-element.471, bf16[2048,64]{1,0:T(8,128)(2,1)S(1)} %get-tuple-element.472, f32[2048]{0:T(1024)S(1)} %get-tuple-element.582, f32[2048]{0:T(1024)S(1)} %get-tuple-element.583, bf16[14336,192]{1,0:T(8,128)(2,1)} %get-tuple-element.473, s32[]{:T(128)S(6)} %select_n.45, ...), kind=kOutput, calls=%fused_computation.47 | convolution fusion | flops 1631846400 | bytes 3425792 | tf_op jit(solution)/shard_map/while/body/eval_jaxpr/cond/branch_1_fun/dot_general | solution.py:77
  231.8 9.8 %conditional.8 = (f32[2048,128]{1,0:T(8,128)}) conditional(s32[]{:T(128)} %convert_element_type.127, f32[2048,128]{1,0:T(8,128)} %get-tuple-element.708, (bf16[2048,64]{1,0:T(8,128)(2,1)S(1)}, s32[]{:T(128)}, bf16[14336,192]{1,0:T(8,128)(2,1)}, f32[2048,128]{1,0:T(8,128)}) %tuple.139), branch_computations={%region_14.14_spmd, %region_15.17_spmd} | conditional | flops 1632628736 | bytes 3966534 | solution.py:81
  231.8 1.7 multiply_reduce_fusion.4
  233.5 8.1 %convolution_add_fusion = f32[2048,128]{1,0:T(8,128)} fusion(f32[2048,128]{1,0:T(8,128)} %get-tuple-element.471, bf16[2048,64]{1,0:T(8,128)(2,1)S(1)} %get-tuple-element.472, f32[2048]{0:T(1024)S(1)} %get-tuple-element.582, f32[2048]{0:T(1024)S(1)} %get-tuple-element.583, bf16[14336,192]{1,0:T(8,128)(2,1)} %get-tuple-element.473, s32[]{:T(128)S(6)} %select_n.45, ...), kind=kOutput, calls=%fused_computation.47 | convolution fusion | flops 1631846400 | bytes 3425792 | tf_op jit(solution)/shard_map/while/body/eval_jaxpr/cond/branch_1_fun/dot_general | solution.py:77
  241.6 2.5 copy.42
  244.2 3.2 %fusion.56 = f32[2048,128]{0,1:T(8,128)} fusion(f32[2048,128]{0,1:T(8,128)S(1)} %copy-done.3, f32[2048,128]{0,1:T(8,128)} %copy.43, f32[2048,128]{0,1:T(8,128)} %copy.42, bf16[2048,256]{1,0:T(8,128)(2,1)S(1)} %copy-done, f32[256,128]{0,1:T(8,128)S(1)} %copy-done.9, f32[128]{0:T(128)S(1)} %copy-done.12, bf16[1,256,256]{2,1,0:T(8,128)(2,1)S(1)} %copy-done.8, ...), kind=kOutput, calls=%fused_computation.58 | convolution fusion | flops 152141824 | bytes 5636608 | tf_op jit(solution)/shard_map/dot_general | solution.py:131
  247.3 2.5 copy.45
  (78 shorter events, 16.0 us)
Async XLA Ops:
  6.5 8.5 %copy-start = (bf16[2048,256]{1,0:T(8,128)(2,1)S(1)}, bf16[2048,256]{1,0:T(8,128)(2,1)}, u32[]{:S(2)}) copy-start(bf16[2048,256]{1,0:T(8,128)(2,1)} %param.29) | copy-start | bytes 3145732
  6.5 22.1 %copy-start.4 = (bf16[2048,64]{0,1:T(8,128)(2,1)S(1)}, bf16[2048,64]{0,1:T(8,128)(2,1)}, u32[]{:S(2)}) copy-start(bf16[2048,64]{0,1:T(8,128)(2,1)} %param.24) | copy-start | bytes 786436
  6.5 9.0 %copy-start.7 = (bf16[1,256,256]{2,1,0:T(8,128)(2,1)S(1)}, bf16[1,256,256]{2,1,0:T(8,128)(2,1)}, u32[]{:S(2)}) copy-start(bf16[1,256,256]{2,1,0:T(8,128)(2,1)} %param.30) | copy-start | bytes 393220
  6.5 22.4 %copy-start.10 = (bf16[1,256,64]{1,2,0:T(8,128)(2,1)S(1)}, bf16[1,256,64]{1,2,0:T(8,128)(2,1)}, u32[]{:S(2)}) copy-start(bf16[1,256,64]{1,2,0:T(8,128)(2,1)} %param.32) | copy-start | bytes 98308
  6.5 117.8 %all-gather.5.cloned.1.call-start = ((), (), s32[]{:S(2)}) async-start(), calls=%async_computation | async-start | bytes 1179648 | tf_op jit(solution)/shard_map/all_gather | solution.py:110
  8.3 1.0 copy-start.2
  9.3 99.5 %copy-start.11 = (s32[1,2048]{1,0:T(1,128)S(1)}, s32[1,2048]{1,0:T(1,128)}, u32[]{:S(2)}) copy-start(s32[1,2048]{1,0:T(1,128)} %param.25) | copy-start | bytes 24580
  9.3 99.5 %copy-start.1 = (f32[2048,128]{1,0:T(8,128)S(1)}, f32[2048,128]{1,0:T(8,128)}, u32[]{:S(2)}) copy-start(f32[2048,128]{1,0:T(8,128)} %param.27) | copy-start | bytes 3145732
  11.3 13.0 %collective-permute-start = (bf16[2048,192]{0,1:T(8,128)(2,1)}, bf16[2048,192]{0,1:T(8,128)(2,1)}, u32[]{:S(2)}, u32[]{:S(2)}) collective-permute-start(bf16[2048,192]{0,1:T(8,128)(2,1)} %pad_maximum_fusion), channel_id=1, source_target_pairs={{0,1},{1,2},{2,3},{3,4},{4,5},{5,6},{6,7},{8,9},{9,10},{10,11},{11... | collective-permute-start | bytes 2359304 | tf_op jit(solution)/shard_map/ppermute | solution.py:12
  15.6 13.4 %copy-start.6 = (bf16[256,128]{1,0:T(8,128)(2,1)}, bf16[256,128]{1,0:T(8,128)(2,1)S(1)}, u32[]{:S(2)}) copy-start(bf16[256,128]{1,0:T(8,128)(2,1)S(1)} %convolution_convert_fusion) | copy-start | bytes 196612
  16.5 38.4 %collective-permute-start.3 = (bf16[2048,192]{0,1:T(8,128)(2,1)}, bf16[2048,192]{0,1:T(8,128)(2,1)}, u32[]{:S(2)}, u32[]{:S(2)}) collective-permute-start(bf16[2048,192]{0,1:T(8,128)(2,1)} %pad_maximum_fusion), channel_id=1, source_target_pairs={{1,0},{2,1},{3,2},{4,3},{5,4},{6,5},{7,6},{9,8},{10,9},{11,10},{12... | collective-permute-start | bytes 2359304 | tf_op jit(solution)/shard_map/ppermute | solution.py:12
  24.3 76.6 %collective-permute-start.1 = (bf16[2048,192]{0,1:T(8,128)(2,1)}, bf16[2048,192]{0,1:T(8,128)(2,1)}, u32[]{:S(2)}, u32[]{:S(2)}) collective-permute-start(bf16[2048,192]{0,1:T(8,128)(2,1)} %collective-permute-done), channel_id=1, source_target_pairs={{0,1},{1,2},{2,3},{3,4},{4,5},{5,6},{6,7},{8,9},{9,10},{10,11},{11... | collective-permute-start | bytes 2359304 | tf_op jit(solution)/shard_map/ppermute | solution.py:12
  54.8 64.1 %collective-permute-start.4 = (bf16[2048,192]{0,1:T(8,128)(2,1)}, bf16[2048,192]{0,1:T(8,128)(2,1)}, u32[]{:S(2)}, u32[]{:S(2)}) collective-permute-start(bf16[2048,192]{0,1:T(8,128)(2,1)} %collective-permute-done.3), channel_id=1, source_target_pairs={{1,0},{2,1},{3,2},{4,3},{5,4},{6,5},{7,6},{9,8},{10,9},{11,10},{12... | collective-permute-start | bytes 2359304 | tf_op jit(solution)/shard_map/ppermute | solution.py:12
  100.9 39.8 %collective-permute-start.2 = (bf16[2048,192]{0,1:T(8,128)(2,1)}, bf16[2048,192]{0,1:T(8,128)(2,1)}, u32[]{:S(2)}, u32[]{:S(2)}) collective-permute-start(bf16[2048,192]{0,1:T(8,128)(2,1)} %collective-permute-done.1), channel_id=1, source_target_pairs={{0,1},{1,2},{2,3},{3,4},{4,5},{5,6},{6,7},{8,9},{9,10},{10,11},{11... | collective-permute-start | bytes 2359304 | tf_op jit(solution)/shard_map/ppermute | solution.py:12
  116.4 18.1 %copy-start.5 = (bf16[4,256,64]{2,1,0:T(8,128)(2,1)S(1)}, bf16[4,256,64]{2,1,0:T(8,128)(2,1)}, u32[]{:S(2)}) copy-start(bf16[4,256,64]{2,1,0:T(8,128)(2,1)} %copy.37) | copy-start | bytes 393220
  116.4 18.1 %copy-start.13 = (s32[1,4]{1,0:T(1,128)S(1)}, s32[1,4]{1,0:T(1,128)}, u32[]{:S(2)}) copy-start(s32[1,4]{1,0:T(1,128)} %param.35) | copy-start | bytes 52
  119.0 33.3 %collective-permute-start.5 = (bf16[2048,192]{0,1:T(8,128)(2,1)}, bf16[2048,192]{0,1:T(8,128)(2,1)}, u32[]{:S(2)}, u32[]{:S(2)}) collective-permute-start(bf16[2048,192]{0,1:T(8,128)(2,1)} %collective-permute-done.4), channel_id=1, source_target_pairs={{1,0},{2,1},{3,2},{4,3},{5,4},{6,5},{7,6},{9,8},{10,9},{11,10},{12... | collective-permute-start | bytes 2359304 | tf_op jit(solution)/shard_map/ppermute | solution.py:12
  154.4 10.4 %copy-start.14 = (s32[1,8]{1,0:T(1,128)S(1)}, s32[1,8]{1,0:T(1,128)}, u32[]{:S(2)}) copy-start(s32[1,8]{1,0:T(1,128)} %param.33) | copy-start | bytes 100
  164.7 79.4 %copy-start.3 = (f32[2048,128]{0,1:T(8,128)S(1)}, f32[2048,128]{0,1:T(8,128)}, u32[]{:S(2)}) copy-start(f32[2048,128]{0,1:T(8,128)} %copy-done.2) | copy-start | bytes 3145732
  164.7 79.4 %copy-start.8 = (bf16[1,256,256]{2,1,0:T(8,128)(2,1)S(1)}, bf16[1,256,256]{2,1,0:T(8,128)(2,1)}, u32[]{:S(2)}) copy-start(bf16[1,256,256]{2,1,0:T(8,128)(2,1)} %param.30) | copy-start | bytes 393220
  164.7 79.4 %copy-start.9 = (f32[256,128]{0,1:T(8,128)S(1)}, f32[256,128]{0,1:T(8,128)}, u32[]{:S(2)}) copy-start(f32[256,128]{0,1:T(8,128)} %copy.39) | copy-start | bytes 393220
  164.7 79.4 %copy-start.12 = (f32[128]{0:T(128)S(1)}, f32[128]{0:T(128)}, u32[]{:S(2)}) copy-start(f32[128]{0:T(128)} %param.28) | copy-start | bytes 1540
Sparse Core Ops, SparseCore 0:
  16.6 24.4 all-gather.4
